TPU v7x, 256 devices: a whole 4x4x8 slice. The times are simulated.
256 devices in a mesh: seq: 16 (over x, y), fsdp: 16 (over z, core).
Axes of the slice: x: 4, y: 4, z: 8, core: 2. Of those that a mesh axis runs over, the one named last changes fastest.
Arguments:
- patches: bfloat16 [16, 8704, 1176], P('fsdp', 'seq'), may hold values from -6 to 6
- send_slot: int32 [16, 272], P('fsdp', 'seq'), may hold values from 0 to 271, as said below
- segments: int32 [16, 272], P('fsdp'), may hold values from 0 to 33, never falling along the last dimension, each value on 1 to 24 neighbouring positions
- stem_weight: bfloat16 [3584, 1176], P('fsdp'), may hold values from -0.1875 to 0.1875
- norm_gain: bfloat16 [3584], P('fsdp'), may hold values from 0.099609375 to 1.8984375
- conv_kernel: bfloat16 [5, 3584], P(None, 'fsdp'), may hold values from -3 to 3
- cotangent: bfloat16 [16, 8704, 3584], P('fsdp', 'seq'), may hold values from -6 to 6
Outputs:
- features: bfloat16 [16, 8704, 3584], P('fsdp', 'seq')
- grad_patches: bfloat16 [16, 8704, 1176], P('fsdp', 'seq')
- grad_weight: bfloat16 [3584, 1176], P('fsdp')
- grad_channels: float32 [6, 3584], P(None, 'fsdp')
Inputs may be any that keep to these rules, and one draw needn't show every extreme that they name: `send_slot`: each row is a permutation of the packed slots. At most 2 frame slots of one device go to one device's packed slots, and every device sends exactly 2 to some device; within a row the number that device s sends to device (s + o) modulo the seq axis size depends on o alone. `segments`: ids never fall along a row; a clip holds 1 to 24 slots, one exactly 24.
All inputs are finite; a program needn't handle non-finite values.
Results may differ from a plain program's by a relative error of at most 0.0056.
Values may be sent and summed in bfloat16 or wider, within the bound.
A program may use at most 192 MiB of HBM per device.

v0:
```python
import math

import jax
import jax.numpy as jnp
from jax import lax
from jax.sharding import PartitionSpec as P

EPSILON = 1e-06


def extended_2(cells, sides, width):
    for axis, dim in sides:
        count = lax.axis_size(axis)
        ends = count - 1
        head = lax.slice_in_dim(cells, 0, width, axis=dim)
        tail = lax.slice_in_dim(cells, cells.shape[dim] - width, cells.shape[dim], axis=dim)
        cells = jnp.concatenate(
            [
                lax.ppermute(tail, axis, [(i, (i + 1) % count) for i in range(ends)]),
                cells,
                lax.ppermute(head, axis, [((i + 1) % count, i) for i in range(ends)]),
            ],
            axis=dim,
        )
    return cells


def slot_mask(segment_row, centre):
    slot_total = segment_row.shape[0]
    safe_centre = jnp.clip(centre, 0, slot_total - 1)
    columns = []
    for offset in range(5):
        neighbour = centre + (offset - 2)
        inside = (neighbour >= 0) & (neighbour < slot_total) & (centre >= 0) & (centre < slot_total)
        same_clip = segment_row[jnp.clip(neighbour, 0, slot_total - 1)] == segment_row[safe_centre]
        columns.append((inside & same_clip).astype(jnp.float32))
    return jnp.stack(columns, axis=1)


def temporal_mix(padded, clip_mask, kernel, slot_total):
    kernel_wide = kernel.astype(jnp.float32)
    result = padded[0:slot_total].astype(jnp.float32) * (
        clip_mask[:, 0][:, None, None] * kernel_wide[0][None, None, :]
    )
    for offset in range(1, 5):
        addend = padded[offset : offset + slot_total].astype(jnp.float32) * (
            clip_mask[:, offset][:, None, None] * kernel_wide[offset][None, None, :]
        )
        result = result + addend
    return result


def temporal_back(slope_padded, mask_padded, kernel, slot_total):
    kernel_wide = kernel.astype(jnp.float32)
    result = jnp.zeros((slot_total,) + slope_padded.shape[1:], jnp.float32)
    for offset in range(5):
        first_row = 4 - offset
        weights_row = (
            mask_padded[first_row : first_row + slot_total, offset][:, None, None]
            * kernel_wide[offset][None, None, :]
        )
        result = (
            result
            + slope_padded[first_row : first_row + slot_total].astype(jnp.float32) * weights_row
        )
    return result


def kernel_sums(slope_blocks, padded, clip_mask, slot_total):
    stacked = []
    for offset in range(5):
        product = jnp.sum(
            slope_blocks.astype(jnp.float32)
            * padded[offset : offset + slot_total].astype(jnp.float32),
            axis=1,
        )
        stacked.append(jnp.sum(product * clip_mask[:, offset][:, None], axis=0))
    return jnp.stack(stacked, axis=0)


def rim_rows(values, margin):
    return extended_2(values, (("seq", 0),), margin)


def shards(patches, send_slot, segments, stem_weight, norm_gain, conv_kernel, cotangent):
    seq_size = lax.axis_size("seq")
    fsdp_size = lax.axis_size("fsdp")
    seq_index = lax.axis_index("seq")
    slot_count = send_slot.shape[1]
    tokens = patches.shape[1]
    slot_rows = tokens // slot_count
    pixel_width = patches.shape[2]
    capacity = 2 * slot_count // seq_size
    destination = send_slot[0]
    owner_index = destination // slot_count
    same_owner = owner_index[:, None] == owner_index[None, :]
    earlier = destination[None, :] < destination[:, None]
    ranking = jnp.sum((same_owner & earlier).astype(jnp.int32), axis=1)
    buffer_row = owner_index * capacity + ranking
    frames = patches[0].reshape(slot_count, slot_rows, pixel_width)
    outbox = (
        jnp.zeros((seq_size * capacity, slot_rows, pixel_width), jnp.bfloat16)
        .at[buffer_row]
        .set(frames)
    )
    position = (
        jnp.full((seq_size * capacity,), -1.0, jnp.float32)
        .at[buffer_row]
        .set((destination % slot_count).astype(jnp.float32))
        .astype(jnp.bfloat16)
    )
    incoming, arrived = (
        lax.all_to_all(outbox, "seq", split_axis=0, concat_axis=0, tiled=True),
        lax.all_to_all(position, "seq", split_axis=0, concat_axis=0, tiled=True),
    )
    arrived_float = arrived.astype(jnp.float32)
    target = jnp.where(arrived_float >= 0.0, arrived_float, float(slot_count)).astype(jnp.int32)
    packed = (
        jnp.zeros((slot_count + 1, slot_rows, pixel_width), jnp.bfloat16)
        .at[target]
        .set(incoming)[:slot_count]
        .reshape(tokens, pixel_width)
    )
    weight_full, gain_low, kernel_full = (
        lax.all_gather(stem_weight, "fsdp", axis=0, tiled=True),
        lax.all_gather(norm_gain, "fsdp", axis=0, tiled=True),
        lax.all_gather(conv_kernel, "fsdp", axis=1, tiled=True),
    )
    gain_wide = gain_low.astype(jnp.float32)
    channels = weight_full.shape[0]
    stem_out = lax.dot_general(
        packed, weight_full, (((1,), (1,)), ((), ())), preferred_element_type=jnp.float32
    )
    inv_rms = lax.rsqrt(jnp.mean(stem_out * stem_out, axis=1, keepdims=True) + EPSILON)
    unit_rows = stem_out * inv_rms
    normed = (unit_rows * gain_wide).astype(jnp.bfloat16)
    segment_row = segments[0]
    centre = seq_index * slot_count + jnp.arange(slot_count, dtype=jnp.int32)
    extended = seq_index * slot_count + jnp.arange(-2, slot_count + 2, dtype=jnp.int32)
    clip_mask = slot_mask(segment_row, centre)
    mask_padded = slot_mask(segment_row, extended)
    padded = rim_rows(normed, 2 * slot_rows).reshape(slot_count + 4, slot_rows, channels)
    mixed_rows = temporal_mix(padded, clip_mask, kernel_full, slot_count).reshape(tokens, channels)
    features = (stem_out + jax.nn.silu(mixed_rows)).astype(jnp.bfloat16)
    upstream_wide = cotangent[0].astype(jnp.float32)
    gate_value = jax.nn.sigmoid(mixed_rows)
    slope_low = (upstream_wide * gate_value * (1.0 + mixed_rows * (1.0 - gate_value))).astype(
        jnp.bfloat16
    )
    slope_padded = rim_rows(slope_low, 2 * slot_rows).reshape(slot_count + 4, slot_rows, channels)
    d_normed = temporal_back(slope_padded, mask_padded, kernel_full, slot_count).reshape(
        tokens, channels
    )
    gated = d_normed * gain_wide
    d_stem = upstream_wide + inv_rms * (
        gated - unit_rows * jnp.mean(gated * unit_rows, axis=1, keepdims=True)
    )
    d_stem_low = d_stem.astype(jnp.bfloat16)
    grad_rows = jnp.dot(d_stem_low, weight_full, preferred_element_type=jnp.float32).astype(
        jnp.bfloat16
    )
    gain_part = jnp.sum(d_normed * unit_rows, axis=0)
    slope_blocks = slope_padded[2 : 2 + slot_count]
    kernel_part = kernel_sums(slope_blocks, padded, clip_mask, slot_count)
    chan_terms = jnp.concatenate([gain_part[None, :], kernel_part], axis=0).T
    weight_block = lax.dot_general(
        d_stem_low, packed, (((0,), (0,)), ((), ())), preferred_element_type=jnp.float32
    )
    grad_shard = lax.psum_scatter(
        jnp.concatenate([weight_block, chan_terms], axis=1), "fsdp", scatter_dimension=0, tiled=True
    )
    summed = lax.psum(grad_shard, "seq")
    grad_scale = 1.0 / math.sqrt(tokens * seq_size * fsdp_size)
    grad_weight = (summed[:, :pixel_width] * grad_scale).astype(jnp.bfloat16)
    grad_channels = (summed[:, pixel_width:] * grad_scale).T
    return (features[None], grad_rows[None], grad_weight, grad_channels)


def solution(mesh):
    in_specs = (
        P("fsdp", "seq", None),
        P("fsdp", "seq"),
        P("fsdp", None),
        P("fsdp", None),
        P("fsdp"),
        P(None, "fsdp"),
        P("fsdp", "seq", None),
    )
    out_specs = (P("fsdp", "seq", None), P("fsdp", "seq", None), P("fsdp", None), P(None, "fsdp"))
    return jax.shard_map(shards, mesh=mesh, in_specs=in_specs, out_specs=out_specs, check_vma=False)
```

profile of v0, /device:TPU:32, one launch (start us, length us, event | category | flops | bytes accessed | tf_op | source)
XLA Modules:
  0.0 470.9 jit_solution(15271871692152045158)
XLA Ops:
  9.3 0.9 convert_reduce_fusion
  12.2 7.0 %all-to-all-start = ((bf16[16,2,1]{1,2,0:T(2,128)(2,1)}), bf16[16,2,1]{1,2,0:T(2,128)(2,1)S(1)}, u32[]{:S(2)}, u32[]{:S(2)}) async-start(bf16[16,2,1]{1,2,0:T(2,128)(2,1)} %all_to_all.12), calls=%async_computation | async-start | bytes 16384 | tf_op jit(solution)/shard_map/all_to_all | solution.py:114
  20.0 0.7 gather_fusion.6
  20.8 0.7 gather_fusion.8
  21.5 0.7 gather_fusion.7
  22.2 0.7 gather_fusion.9
  23.0 18.3 %all-gather = bf16[16,224,5]{1,2,0:T(8,128)(2,1)S(1)} all-gather(bf16[1,224,5]{1,2,0:T(8,128)(2,1)} %bitcast.126), channel_id=1, replica_groups=mesh['seq'=16,'fsdp'=16] {'fsdp'}, dimensions={0}, use_global_device_ids=true | all-gather | bytes 38080 | tf_op jit(solution)/shard_map/all_gather | solution.py:127
  45.6 0.8 broadcast_multiply_fusion
  46.4 0.9 broadcast_multiply_fusion.1
  47.4 1.8 broadcast_in_dim.19
  49.2 5.8 %scatter_fusion = bf16[32,32,1176]{2,1,0:T(8,128)(2,1)} fusion(bf16[32,32,1176]{2,1,0:T(8,128)(2,1)} %broadcast_in_dim.19, s32[17]{0:T(128)S(1)} %fusion.26, bf16[17,32,1176]{2,1,0:T(8,128)(2,1)S(1)} %bitcast.120), kind=kCustom, calls=%fused_computation.11 | custom fusion | bytes 3838532 | tf_op jit(solution)/shard_map/scatter | solution.py:104
  55.0 7.3 %all-to-all-start.1 = ((bf16[32,32,1176]{2,1,0:T(8,128)(2,1)}), bf16[32,32,1176]{2,1,0:T(8,128)(2,1)}, u32[]{:S(2)}, u32[]{:S(2)}) async-start(bf16[32,32,1176]{2,1,0:T(8,128)(2,1)} %scatter_fusion), calls=%async_computation.1 | async-start | bytes 5242880 | tf_op jit(solution)/shard_map/all_to_all | solution.py:113
  63.9 24.1 %all-reduce = bf16[3584]{0:T(1024)(128)(2,1)S(1)} all-reduce(bf16[3584]{0:T(1024)(128)(2,1)S(1)} %dynamic-update-slice), channel_id=1, replica_groups=mesh['seq'=16,'fsdp'=16] {'fsdp'}, use_global_device_ids=true, to_apply=%add | all-reduce | flops 3584 | bytes 14336
  88.0 1.0 broadcast_multiply_fusion.2
  89.0 1.0 broadcast_multiply_fusion.3
  90.1 8.8 %all-to-all-done.1 = bf16[32,32,1176]{2,1,0:T(8,128)(2,1)} async-done(((bf16[32,32,1176]{2,1,0:T(8,128)(2,1)}), bf16[32,32,1176]{2,1,0:T(8,128)(2,1)}, u32[]{:S(2)}, u32[]{:S(2)}) %all-to-all-start.1) | async-done | bytes 2408480 | tf_op jit(solution)/shard_map/all_to_all | solution.py:113
  99.1 4.2 scatter_fusion.1
  103.4 8.0 %multiply_reduce_fusion.2 = (f32[544]{0:T(1024)S(1)}, f32[544,3584]{1,0:T(8,128)S(1)}) fusion(bf16[544,1176]{1,0:T(8,128)(2,1)S(1)} %bitcast.121, bf16[3584,1176]{1,0:T(8,128)(2,1)} %all-gather.3.cloned.1.call-done), kind=kOutput, calls=%fused_computation.47 | convolution fusion | flops 4589583872 | bytes 17510016 | tf_op jit(solution)/shard_map/dot_general | solution.py:131
  111.5 1.3 multiply_convert_fusion
  112.9 1.6 collective-permute-start.1
  114.5 4.8 %collective-permute-start = (bf16[64,3584]{1,0:T(8,128)(2,1)S(1)}, bf16[64,3584]{1,0:T(8,128)(2,1)S(1)}, u32[]{:S(2)}, u32[]{:S(2)}) collective-permute-start(bf16[64,3584]{1,0:T(8,128)(2,1)S(1)} %get-tuple-element.46), channel_id=1, source_target_pairs={{0,16},{16,32},{32,48},{48,64},{64,80},{80,96},{96,112},{112,128},... | collective-permute-start | bytes 1376264 | tf_op jit(solution)/shard_map/ppermute | solution.py:19
  119.3 0.9 broadcast_multiply_fusion.4
  120.2 5.9 %collective-permute-done.1 = bf16[64,3584]{1,0:T(8,128)(2,1)S(1)} collective-permute-done((bf16[64,3584]{1,0:T(8,128)(2,1)S(1)}, bf16[64,3584]{1,0:T(8,128)(2,1)S(1)}, u32[]{:S(2)}, u32[]{:S(2)}) %collective-permute-start.1) | collective-permute-done | bytes 458784 | tf_op jit(solution)/shard_map/ppermute | solution.py:21
  126.1 1.3 collective-permute-done
  127.4 8.3 %convert_multiply_fusion = (f32[544,3584]{1,0:T(8,128)}, bf16[544,3584]{1,0:T(8,128)(2,1)S(1)}, f32[544,3584]{1,0:T(8,128)}) fusion(bf16[64,3584]{1,0:T(8,128)(2,1)S(1)} %collective-permute-done.1, bf16[544,3584]{1,0:T(8,128)(2,1)S(1)} %multiply_convert_fusion, bf16[1,544,3584]{2,1,0:T(8,128)(2,1)S(1)} %copy-done.5, f32[17,3584]{1,0:T(8,128)S(1)} %copy-done.7, ...), kind=kLoop, calls=%fused_computation.13 | loop fusion | flops 74088448 | bytes 29431808 | tf_op jit(solution)/shard_map/mul | solution.py:73
  135.7 1.9 copy-done.3
  137.6 0.8 fusion.45
  138.5 5.5 %collective-permute-start.3 = (bf16[64,3584]{1,0:T(8,128)(2,1)}, bf16[64,3584]{1,0:T(8,128)(2,1)}, u32[]{:S(2)}, u32[]{:S(2)}) collective-permute-start(bf16[64,3584]{1,0:T(8,128)(2,1)} %get-tuple-element.45), channel_id=1, source_target_pairs={{0,16},{16,32},{32,48},{48,64},{64,80},{80,96},{96,112},{112,128},... | collective-permute-start | bytes 1376264 | tf_op jit(solution)/shard_map/ppermute | solution.py:19
  144.0 1.5 collective-permute-start.2
  145.5 15.1 %convert_multiply_fusion.1 = (f32[544,3584]{1,0:T(8,128)}, f32[544,3584]{1,0:T(8,128)}, f32[544,3584]{1,0:T(8,128)}, f32[544,3584]{1,0:T(8,128)}) fusion(bf16[544,3584]{1,0:T(8,128)(2,1)} %copy-done.3, bf16[64,3584]{1,0:T(8,128)(2,1)S(1)} %collective-permute-done.1, bf16[544,3584]{1,0:T(8,128)(2,1)} %copy-done.4, bf16[64,3584]{1,0:T(8,128)(2,1)S(1)} %collective-permute-done), kind=kLoop, calls=%fused_computation.14 | loop fusion | flops 35094528 | bytes 39911424 | tf_op jit(solution)/shard_map/mul | solution.py:73
  160.6 4.3 reduce_sum.133
  165.1 4.4 reduce_sum.135
  169.6 4.4 reduce_sum.137
  174.1 4.4 reduce_sum.139
  178.6 4.4 reduce_sum.141
  183.1 10.2 %fusion.9 = f32[544,3584]{1,0:T(8,128)S(1)} fusion(bf16[544,3584]{1,0:T(8,128)(2,1)} %copy-done.3, bf16[64,3584]{1,0:T(8,128)(2,1)} %collective-permute-done.3, bf16[64,3584]{1,0:T(8,128)(2,1)} %collective-permute-done.2, f32[17,3584]{1,0:T(8,128)S(1)} %get-tuple-element.56, f32[17,3584]{1,0:T(8,128)} %get-tuple-element.54, ...), kind=kLoop, calls=%fused_computation.36 | loop fusion | flops 50692096 | bytes 13834240 | tf_op jit(solution)/shard_map/add | solution.py:63
  193.4 2.1 multiply_reduce_fusion
  195.5 9.9 %fusion.6 = (bf16[544,3584]{1,0:T(8,128)(2,1)}, bf16[1,544,3584]{2,1,0:T(8,128)(2,1)}) fusion(f32[544,3584]{1,0:T(8,128)S(1)} %fusion.9, f32[544,3584]{1,0:T(8,128)S(1)} %bitcast.114, bf16[1,544,3584]{2,1,0:T(8,128)(2,1)} %param.13, f32[544]{0:T(1024)S(1)} %broadcast_multiply_fusion.10, f32[3584]{0:T(1024)S(1)} %convert_element_type.185, ...), kind=kLoop, calls=%fused_computation.33 | loop fusion | flops 27295744 | bytes 35113216 | tf_op jit(solution)/shard_map/convert_element_type | solution.py:158
  205.4 12.7 %fusion.47 = f32[3584,1176]{0,1:T(8,128)} fusion(bf16[544,3584]{1,0:T(8,128)(2,1)} %get-tuple-element.42, bf16[544,1176]{1,0:T(8,128)(2,1)S(1)} %bitcast.122), kind=kOutput, calls=%fused_computation.172 | convolution fusion | flops 4585684992 | bytes 22038016 | tf_op jit(solution)/shard_map/dot_general | solution.py:166
  218.2 11.5 %pad_maximum_fusion = f32[3584,1182]{0,1:T(8,128)} fusion(f32[3584,6]{0,1:T(8,128)S(1)} %bitcast.123, f32[3584,1176]{0,1:T(8,128)} %fusion.47), kind=kLoop, calls=%fused_computation.19 | loop fusion | flops 4236288 | bytes 33890304 | tf_op jit(solution)/shard_map/concatenate | solution.py:170
  229.7 18.8 %copy.23 = f32[3584,1182]{1,0:T(8,128)} copy(f32[3584,1182]{0,1:T(8,128)} %pad_maximum_fusion) | data formatting | bytes 33890304
  248.6 109.6 %reduce-scatter.4.cloned.1.call-done = f32[224,1182]{1,0:T(8,128)} async-done(((f32[3584,1182]{1,0:T(8,128)}), f32[224,1182]{1,0:T(8,128)}) %reduce-scatter.4.cloned.1.call-update) | async-done | bytes 1059088
  358.2 2.7 copy.24
  360.9 10.4 %fusion.16 = bf16[1,544,1176]{2,1,0:T(8,128)(2,1)} fusion(bf16[544,3584]{1,0:T(8,128)(2,1)} %get-tuple-element.42, bf16[3584,1176]{1,0:T(8,128)(2,1)} %all-gather.3.cloned.1.call-done), kind=kOutput, calls=%fused_computation.66 | convolution fusion | flops 4586324992 | bytes 13608448 | tf_op jit(solution)/shard_map/dot_general | solution.py:159
  371.3 89.3 %all-reduce.3.cloned.1.call-done = f32[224,1182]{0,1:T(8,128)} async-done(((f32[224,1182]{0,1:T(8,128)}), f32[224,1182]{0,1:T(8,128)}) %all-reduce.3.cloned.1.call-update) | async-done | bytes 1059088 | tf_op jit(solution)/shard_map/psum | solution.py:172
  460.6 1.4 fusion.17
  462.0 1.0 copy.22
  463.1 1.3 fusion.18
  (107 shorter events, 11.4 us)
Async XLA Ops:
  7.2 12.1 %copy-start = (s32[1,272]{1,0:T(1,128)S(1)}, s32[1,272]{1,0:T(1,128)}, u32[]{:S(2)}) copy-start(s32[1,272]{1,0:T(1,128)} %param.9) | copy-start | bytes 3268
  7.2 42.0 %copy-start.6 = (bf16[1,544,1176]{2,1,0:T(8,128)(2,1)S(1)}, bf16[1,544,1176]{2,1,0:T(8,128)(2,1)}, u32[]{:S(2)}) copy-start(bf16[1,544,1176]{2,1,0:T(8,128)(2,1)} %param.7) | copy-start | bytes 3838468
  7.2 96.2 %all-gather.3.cloned.1.call-start = ((), (), s32[]{:S(2)}) async-start(), calls=%async_computation.3 | async-start | bytes 9748480 | tf_op jit(solution)/shard_map/all_gather | solution.py:125
  12.2 42.8 %all-to-all-start = ((bf16[16,2,1]{1,2,0:T(2,128)(2,1)}), bf16[16,2,1]{1,2,0:T(2,128)(2,1)S(1)}, u32[]{:S(2)}, u32[]{:S(2)}) async-start(bf16[16,2,1]{1,2,0:T(2,128)(2,1)} %all_to_all.12), calls=%async_computation | async-start | bytes 16384 | tf_op jit(solution)/shard_map/all_to_all | solution.py:114
  42.2 20.2 %copy-start.12 = (u32[256]{0:T(256)S(1)}, u32[256]{0:T(256)}, u32[]{:S(2)}) copy-start(u32[256]{0:T(256)} %constant.79) | copy-start | bytes 3076
  42.2 21.5 %copy-start.11 = (bf16[224]{0:T(256)(128)(2,1)S(1)}, bf16[224]{0:T(256)(128)(2,1)}, u32[]{:S(2)}) copy-start(bf16[224]{0:T(256)(128)(2,1)} %param.11) | copy-start | bytes 1348
  55.0 44.0 %all-to-all-start.1 = ((bf16[32,32,1176]{2,1,0:T(8,128)(2,1)}), bf16[32,32,1176]{2,1,0:T(8,128)(2,1)}, u32[]{:S(2)}, u32[]{:S(2)}) async-start(bf16[32,32,1176]{2,1,0:T(8,128)(2,1)} %scatter_fusion), calls=%async_computation.1 | async-start | bytes 5242880 | tf_op jit(solution)/shard_map/all_to_all | solution.py:113
  62.3 295.9 %reduce-scatter.4.cloned.1.call-start = ((), (), s32[]{:S(2)}) async-start(), calls=%async_computation.5 | async-start | bytes 19496960
  111.4 24.3 %copy-start.2 = (f32[544,3584]{1,0:T(8,128)}, f32[544,3584]{1,0:T(8,128)S(1)}, u32[]{:S(2)}) copy-start(f32[544,3584]{1,0:T(8,128)S(1)} %get-tuple-element.69) | copy-start | bytes 23396356
  111.5 15.9 %copy-start.5 = (bf16[1,544,3584]{2,1,0:T(8,128)(2,1)S(1)}, bf16[1,544,3584]{2,1,0:T(8,128)(2,1)}, u32[]{:S(2)}) copy-start(bf16[1,544,3584]{2,1,0:T(8,128)(2,1)} %param.13) | copy-start | bytes 11698180
  111.5 15.9 %copy-start.7 = (f32[17,3584]{1,0:T(8,128)S(1)}, f32[17,3584]{1,0:T(8,128)}, u32[]{:S(2)}) copy-start(f32[17,3584]{1,0:T(8,128)} %get-tuple-element.57) | copy-start | bytes 731140
  111.5 15.9 %copy-start.8 = (f32[17,3584]{1,0:T(8,128)S(1)}, f32[17,3584]{1,0:T(8,128)}, u32[]{:S(2)}) copy-start(f32[17,3584]{1,0:T(8,128)} %get-tuple-element.55) | copy-start | bytes 731140
  111.5 15.9 %copy-start.9 = (f32[17,3584]{1,0:T(8,128)S(1)}, f32[17,3584]{1,0:T(8,128)}, u32[]{:S(2)}) copy-start(f32[17,3584]{1,0:T(8,128)} %get-tuple-element.53) | copy-start | bytes 731140
  111.5 15.9 %copy-start.10 = (f32[17,3584]{1,0:T(8,128)S(1)}, f32[17,3584]{1,0:T(8,128)}, u32[]{:S(2)}) copy-start(f32[17,3584]{1,0:T(8,128)} %get-tuple-element.51) | copy-start | bytes 731140
  112.8 22.9 %copy-start.4 = (bf16[544,3584]{1,0:T(8,128)(2,1)}, bf16[544,3584]{1,0:T(8,128)(2,1)S(1)}, u32[]{:S(2)}) copy-start(bf16[544,3584]{1,0:T(8,128)(2,1)S(1)} %multiply_convert_fusion) | copy-start | bytes 11698180
  112.9 13.1 %collective-permute-start.1 = (bf16[64,3584]{1,0:T(8,128)(2,1)S(1)}, bf16[64,3584]{1,0:T(8,128)(2,1)S(1)}, u32[]{:S(2)}, u32[]{:S(2)}) collective-permute-start(bf16[64,3584]{1,0:T(8,128)(2,1)S(1)} %get-tuple-element.47), channel_id=1, source_target_pairs={{16,0},{32,16},{48,32},{64,48},{80,64},{96,80},{112,96},{128,112},... | collective-permute-start | bytes 1376264 | tf_op jit(solution)/shard_map/ppermute | solution.py:21
  114.5 12.9 %collective-permute-start = (bf16[64,3584]{1,0:T(8,128)(2,1)S(1)}, bf16[64,3584]{1,0:T(8,128)(2,1)S(1)}, u32[]{:S(2)}, u32[]{:S(2)}) collective-permute-start(bf16[64,3584]{1,0:T(8,128)(2,1)S(1)} %get-tuple-element.46), channel_id=1, source_target_pairs={{0,16},{16,32},{32,48},{48,64},{64,80},{80,96},{96,112},{112,128},... | collective-permute-start | bytes 1376264 | tf_op jit(solution)/shard_map/ppermute | solution.py:19
  135.7 1.9 copy-start.3
  138.5 44.6 %collective-permute-start.3 = (bf16[64,3584]{1,0:T(8,128)(2,1)}, bf16[64,3584]{1,0:T(8,128)(2,1)}, u32[]{:S(2)}, u32[]{:S(2)}) collective-permute-start(bf16[64,3584]{1,0:T(8,128)(2,1)} %get-tuple-element.45), channel_id=1, source_target_pairs={{0,16},{16,32},{32,48},{48,64},{64,80},{80,96},{96,112},{112,128},... | collective-permute-start | bytes 1376264 | tf_op jit(solution)/shard_map/ppermute | solution.py:19
  144.0 39.1 %collective-permute-start.2 = (bf16[64,3584]{1,0:T(8,128)(2,1)S(1)}, bf16[64,3584]{1,0:T(8,128)(2,1)}, u32[]{:S(2)}, u32[]{:S(2)}) collective-permute-start(bf16[64,3584]{1,0:T(8,128)(2,1)S(1)} %get-tuple-element.44), channel_id=1, source_target_pairs={{16,0},{32,16},{48,32},{64,48},{80,64},{96,80},{112,96},{128,112},... | collective-permute-start | bytes 1376264 | tf_op jit(solution)/shard_map/ppermute | solution.py:21
  182.9 10.4 %slice-start = ((s8[7798784]{0:T(1024)(128)(4,1)}), s8[4194304]{0:T(1024)(128)(4,1)S(1)}, s32[]{:S(2)}) async-start(s8[7798784]{0:T(1024)(128)(4,1)} %bitcast.113), calls=%async_computation.6 | async-start | bytes 8388608
  183.1 10.3 %slice-start.1 = ((s8[7798784]{0:T(1024)(128)(4,1)}), s8[3604480]{0:T(1024)(128)(4,1)S(1)}, s32[]{:S(2)}) async-start(s8[7798784]{0:T(1024)(128)(4,1)} %bitcast.113), calls=%async_computation.7 | async-start | bytes 7208960
  248.6 212.0 %all-reduce.3.cloned.1.call-start = ((), (), s32[]{:S(2)}) async-start(), calls=%async_computation.4 | async-start | bytes 2424832 | tf_op jit(solution)/shard_map/psum | solution.py:172
  360.9 103.5 %copy-start.1 = (s32[1,272]{1,0:T(1,128)S(1)}, s32[1,272]{1,0:T(1,128)}, u32[]{:S(2)}) copy-start(s32[1,272]{1,0:T(1,128)} %param.9) | copy-start | bytes 3268
Sparse Core Ops, SparseCore 0:
  9.9 60.7 all-gather.2
  248.7 109.4 reduce-scatter.3
  361.5 99.0 all-reduce.2
where the time goes:
time: 472 us; the launch traced here: 471 us
  waiting for transfers between devices  216 us (46%)
  other arithmetic  91.6 us (19%)
  local copies, waits for them, and re-layouts  47.3 us (10%)
  blocking collectives  42.4 us (9%)
  matrix products  31.2 us (7%)
  starting transfers between devices  27.9 us (6%)
  between operations  15 us (3%)
    unnamed x4, waiting for transfers between devices  110 us
    psum x1, waiting for transfers between devices, shards(): summed = lax.psum(grad_shard, 'seq')  89.3 us
    unnamed x36, local copies, waits for them, and re-layouts  25.4 us
    unnamed x1, blocking collectives  24.1 us
    mul x2, other arithmetic, kernel_sums(): slope_blocks.astype(jnp.float32)  23.4 us
    reduce_sum x5, other arithmetic, kernel_sums(): jnp.sum(slope_blocks.astype(jnp.float32) * padded[offset:offset + slot_to...  21.8 us
    all_gather x1, blocking collectives, shards(): lax.all_gather(conv_kernel, 'fsdp', axis=1, tiled=True)  18.3 us
    dot_general x1, matrix products, shards(): lax.dot_general(d_stem_low, packed, (((0,), (0,)), ((), ())), preferred_e...  12.7 us
  transfers between devices with their start and end apart: 9, of which 5 were waited for; matrix products, arithmetic and copies ran while one was open for 16% of the time, Pallas kernels for 0%

commit v1 on v0

--- a/solution.py
+++ b/solution.py
@@ -6,6 +6,10 @@
 from jax.sharding import PartitionSpec as P
 
 EPSILON = 1e-06
+
+
+def pl_ceil(total, step):
+    return -(-total // step)
 
 
 def extended_2(cells, sides, width):
@@ -121,11 +125,13 @@
         .set(incoming)[:slot_count]
         .reshape(tokens, pixel_width)
     )
-    weight_full, gain_low, kernel_full = (
-        lax.all_gather(stem_weight, "fsdp", axis=0, tiled=True),
-        lax.all_gather(norm_gain, "fsdp", axis=0, tiled=True),
-        lax.all_gather(conv_kernel, "fsdp", axis=1, tiled=True),
-    )
+    extras = jnp.concatenate([norm_gain[:, None], conv_kernel.T], axis=1)
+    shard_ext = jnp.concatenate([stem_weight, extras], axis=1)
+    gathered = lax.all_gather(shard_ext, "fsdp", axis=0, tiled=True)
+    weight_full = gathered[:, :pixel_width]
+    channel_low = gathered[:, pixel_width:].T
+    gain_low = channel_low[0]
+    kernel_full = channel_low[1:]
     gain_wide = gain_low.astype(jnp.float32)
     channels = weight_full.shape[0]
     stem_out = lax.dot_general(
@@ -164,15 +170,23 @@
     kernel_part = kernel_sums(slope_blocks, padded, clip_mask, slot_count)
     chan_terms = jnp.concatenate([gain_part[None, :], kernel_part], axis=0).T
     weight_block = lax.dot_general(
-        d_stem_low, packed, (((0,), (0,)), ((), ())), preferred_element_type=jnp.float32
-    )
-    grad_shard = lax.psum_scatter(
-        jnp.concatenate([weight_block, chan_terms], axis=1), "fsdp", scatter_dimension=0, tiled=True
-    )
-    summed = lax.psum(grad_shard, "seq")
+        d_stem_low,
+        jnp.pad(packed, ((0, 0), (0, 6))),
+        (((0,), (0,)), ((), ())),
+        preferred_element_type=jnp.float32,
+    )
+    total_block = weight_block + jnp.pad(chan_terms, ((0, 0), (pixel_width, 0)))
+    panel = channels // fsdp_size
+    panel_padded = 16 * seq_size * pl_ceil(panel, 16 * seq_size)
+    stacked = jnp.pad(
+        total_block.reshape(fsdp_size, panel, pixel_width + 6),
+        ((0, 0), (0, panel_padded - panel), (0, 0)),
+    ).reshape(fsdp_size * panel_padded, pixel_width + 6)
+    piece = lax.psum_scatter(stacked, ("fsdp", "seq"), scatter_dimension=0, tiled=True)
     grad_scale = 1.0 / math.sqrt(tokens * seq_size * fsdp_size)
-    grad_weight = (summed[:, :pixel_width] * grad_scale).astype(jnp.bfloat16)
-    grad_channels = (summed[:, pixel_width:] * grad_scale).T
+    summed = lax.all_gather(piece * grad_scale, "seq", axis=0, tiled=True)[:panel]
+    grad_weight = summed[:, :pixel_width].astype(jnp.bfloat16)
+    grad_channels = summed[:, pixel_width:].T
     return (features[None], grad_rows[None], grad_weight, grad_channels)
 
 

time: 472 us -> 1610 us (3.41)
  waiting for transfers between devices: 216 us -> 1380 us
  blocking collectives: 42.4 us -> 0 us
  local copies, waits for them, and re-layouts: 47.3 us -> 71.6 us
    reduce_scatter x0 -> x1, waiting for transfers between devices: none -> 1230 us  [shards(): lax.psum_scatter(stacked, ('fsdp', 'seq'), scatter_dimension=0, tiled=True)]
    unnamed x4 -> x3, waiting for transfers between devices: 110 us -> 0.05 us
    all_gather x1 -> x2, waiting for transfers between devices: 0.02 us -> 108 us  [the longest x1 108 us: shards(): lax.all_gather(piece * grad_scale, 'seq', axis=0, tiled=True)[:panel]]
    psum x1 -> x0, waiting for transfers between devices: 89.3 us -> none  [shards(): summed = lax.psum(grad_shard, 'seq')]
    unnamed x36 -> x17, local copies, waits for them, and re-layouts: 25.4 us -> 0.73 us
    unnamed x1 -> x0, blocking collectives: 24.1 us -> none
    all_to_all x1, waiting for transfers between devices: 8.82 us -> 28.8 us  [shards(): lax.all_to_all(outbox, 'seq', split_axis=0, concat_axis=0, tiled=True)]
    add x0 -> x1, local copies, waits for them, and re-layouts: none -> 18.8 us  [shards(): total_block = weight_block + jnp.pad(chan_terms, ((0, 0), (pixel_width, 0)))]
  transfers between devices with their start and end apart: 9 -> 9, of which waited for: 5 -> 5; matrix products, arithmetic and copies ran while one was open for 16% -> 4% of each run, Pallas kernels for 0% -> 0%
where the time goes in v1:
time: 1610 us
  waiting for transfers between devices  1380 us (86%)
  other arithmetic  89.6 us (6%)
  local copies, waits for them, and re-layouts  71.6 us (4%)
  matrix products  29.6 us (2%)
  starting transfers between devices  25.2 us (2%)
    reduce_scatter x1, waiting for transfers between devices, shards(): lax.psum_scatter(stacked, ('fsdp', 'seq'), scatter_dimension=0, tiled=True)  1230 us
    all_gather x1, waiting for transfers between devices, shards(): lax.all_gather(piece * grad_scale, 'seq', axis=0, tiled=True)[:panel]  108 us
    mul x2, other arithmetic, kernel_sums(): slope_blocks.astype(jnp.float32)  34.7 us
  transfers between devices with their start and end apart: 9, of which 5 were waited for; matrix products, arithmetic and copies ran while one was open for 4% of the time, Pallas kernels for 0%

profile of v1, /device:TPU:32, one launch (start us, length us, event | category | flops | bytes accessed | tf_op | source)
XLA Modules:
  0.0 1607.2 jit_solution(15183071175365913867)
XLA Ops:
  7.2 0.7 broadcast_in_dim.26
  8.0 0.8 copy.34
  8.8 1.9 concatenate.24
  12.1 0.9 convert_reduce_fusion.1
  15.0 7.0 all-to-all-start
  22.3 1.8 broadcast_in_dim.21
  24.1 6.9 scatter_fusion
  31.0 7.2 all-to-all-start.1
  39.0 0.7 gather_fusion.5
  39.7 0.7 gather_fusion.1
  40.4 0.7 gather_fusion.2
  44.0 0.7 gather_fusion.8
  45.9 28.8 %all-to-all-done.1 = bf16[32,32,1176]{2,1,0:T(8,128)(2,1)} async-done(((bf16[32,32,1176]{2,1,0:T(8,128)(2,1)}), bf16[32,32,1176]{2,1,0:T(8,128)(2,1)}, u32[]{:S(2)}, u32[]{:S(2)}) %all-to-all-start.1) | async-done | bytes 2408480 | tf_op jit(solution)/shard_map/all_to_all | solution.py:117
  74.8 4.6 scatter_fusion.1
  79.6 1.6 slice_bitcast_fusion
  81.9 4.3 slice_reduce_fusion.4
  86.2 5.5 multiply_reduce_fusion.2
  91.7 1.3 multiply_convert_fusion
  93.1 2.9 collective-permute-start
  96.0 1.3 collective-permute-start.1
  97.4 0.8 broadcast_multiply_fusion
  98.3 0.9 broadcast_multiply_fusion.1
  99.1 0.9 broadcast_multiply_fusion.2
  100.0 0.9 broadcast_multiply_fusion.3
  100.9 2.1 collective-permute-done
  103.0 4.3 collective-permute-done.1
  107.3 19.6 %convert_multiply_fusion = (f32[544,3584]{1,0:T(8,128)}, bf16[544,3584]{1,0:T(8,128)(2,1)}, f32[544,3584]{1,0:T(8,128)}) fusion(bf16[64,3584]{1,0:T(8,128)(2,1)S(1)} %collective-permute-done.1, bf16[544,3584]{1,0:T(8,128)(2,1)S(1)} %multiply_convert_fusion, bf16[1,544,3584]{2,1,0:T(8,128)(2,1)S(1)} %copy-done.4, f32[17,3584]{1,0:T(8,128)S(1)} %get-tuple-element.57, ...), kind=kLoop, calls=%fused_computation.13 | loop fusion | flops 74088448 | bytes 29431808 | tf_op jit(solution)/shard_map/mul | solution.py:77
  126.9 4.3 reduce_sum.141
  131.4 2.0 fusion.54
  133.3 1.3 collective-permute-start.2
  134.6 5.4 collective-permute-start.3
  140.0 15.1 convert_multiply_fusion.1
  155.1 4.3 reduce_sum.139
  159.6 4.4 reduce_sum.137
  164.1 4.4 reduce_sum.133
  168.6 4.4 reduce_sum.135
  173.2 10.2 fusion.13
  183.5 2.1 multiply_reduce_fusion
  185.6 9.6 fusion.10
  195.3 13.7 pad_add_fusion
  209.1 18.8 %copy.35 = f32[3584,1182]{1,0:T(8,128)} copy(f32[3584,1182]{0,1:T(8,128)} %pad_add_fusion) | data formatting | bytes 33890304 | tf_op jit(solution)/shard_map/add | solution.py:178
  227.9 15.3 pad.14
  243.2 1233.8 %reduce-scatter.4.cloned.1.call-done = f32[16,1182]{1,0:T(8,128)} async-done(((f32[4096,1182]{1,0:T(8,128)}), f32[16,1182]{1,0:T(8,128)}) %reduce-scatter.4.cloned.1.call-update) | async-done | bytes 75664 | tf_op jit(solution)/shard_map/reduce_scatter | solution.py:185
  1477.0 1.5 broadcast_multiply_fusion.10
  1478.6 10.4 fusion.23
  1489.0 107.6 %all-gather.5.cloned.1.call-done = f32[256,1182]{1,0:T(8,128)} async-done(((f32[16,1182]{1,0:T(8,128)}), f32[256,1182]{1,0:T(8,128)}) %all-gather.5.cloned.1.call-update) | async-done | bytes 1210384 | tf_op jit(solution)/shard_map/all_gather | solution.py:187
  1596.6 1.0 slice_bitcast_fusion.1
  1598.3 2.1 slice.292
  (91 shorter events, 11.0 us)
Async XLA Ops:
  7.2 31.1 %copy-start = (s32[1,272]{1,0:T(1,128)S(1)}, s32[1,272]{1,0:T(1,128)}, u32[]{:S(2)}) copy-start(s32[1,272]{1,0:T(1,128)} %param.9) | copy-start | bytes 3268
  7.2 72.4 %all-gather.3.cloned.1.call-start = ((), (), s32[]{:S(2)}) async-start(), calls=%async_computation.3 | async-start | bytes 9748480 | tf_op jit(solution)/shard_map/all_gather | solution.py:130
  15.0 15.9 all-to-all-start
  31.0 43.7 %all-to-all-start.1 = ((bf16[32,32,1176]{2,1,0:T(8,128)(2,1)}), bf16[32,32,1176]{2,1,0:T(8,128)(2,1)}, u32[]{:S(2)}, u32[]{:S(2)}) async-start(bf16[32,32,1176]{2,1,0:T(8,128)(2,1)} %scatter_fusion), calls=%async_computation.1 | async-start | bytes 5242880 | tf_op jit(solution)/shard_map/all_to_all | solution.py:117
  38.2 1438.8 %reduce-scatter.4.cloned.1.call-start = ((), (), s32[]{:S(2)}) async-start(), calls=%async_computation.5 | async-start | bytes 21053440 | tf_op jit(solution)/shard_map/reduce_scatter | solution.py:185
  79.6 6.7 copy-start.5
  91.7 7.5 copy-start.2
  91.7 15.6 copy-start.4
  93.0 33.8 %copy-start.3 = (bf16[544,3584]{1,0:T(8,128)(2,1)}, bf16[544,3584]{1,0:T(8,128)(2,1)S(1)}, u32[]{:S(2)}) copy-start(bf16[544,3584]{1,0:T(8,128)(2,1)S(1)} %multiply_convert_fusion) | copy-start | bytes 11698180
  93.1 9.9 collective-permute-start
  96.0 11.3 collective-permute-start.1
  133.3 39.8 %collective-permute-start.2 = (bf16[64,3584]{1,0:T(8,128)(2,1)}, bf16[64,3584]{1,0:T(8,128)(2,1)}, u32[]{:S(2)}, u32[]{:S(2)}) collective-permute-start(bf16[64,3584]{1,0:T(8,128)(2,1)} %get-tuple-element.44), channel_id=1, source_target_pairs={{16,0},{32,16},{48,32},{64,48},{80,64},{96,80},{112,96},{128,112},... | collective-permute-start | bytes 1376264 | tf_op jit(solution)/shard_map/ppermute | solution.py:25
  134.6 38.5 %collective-permute-start.3 = (bf16[64,3584]{1,0:T(8,128)(2,1)S(1)}, bf16[64,3584]{1,0:T(8,128)(2,1)}, u32[]{:S(2)}, u32[]{:S(2)}) collective-permute-start(bf16[64,3584]{1,0:T(8,128)(2,1)S(1)} %get-tuple-element.45), channel_id=1, source_target_pairs={{0,16},{16,32},{32,48},{48,64},{64,80},{80,96},{96,112},{112,128},... | collective-permute-start | bytes 1376264 | tf_op jit(solution)/shard_map/ppermute | solution.py:23
  173.0 10.4 slice-start
  173.2 10.3 slice-start.1
  243.1 1353.5 %all-gather.5.cloned.1.call-start = ((), (), s32[]{:S(2)}) async-start(), calls=%async_computation.4 | async-start | bytes 1392640 | tf_op jit(solution)/shard_map/all_gather | solution.py:187
  1478.6 121.8 %copy-start.1 = (s32[1,272]{1,0:T(1,128)S(1)}, s32[1,272]{1,0:T(1,128)}, u32[]{:S(2)}) copy-start(s32[1,272]{1,0:T(1,128)} %param.9) | copy-start | bytes 3268
Sparse Core Ops, SparseCore 0:
  10.9 60.3 all-gather.2
  243.3 1233.7 reduce-scatter.3
  1480.1 116.4 all-gather.4

commit v2 on v1

--- a/solution.py
+++ b/solution.py
@@ -3,13 +3,107 @@
 import jax
 import jax.numpy as jnp
 from jax import lax
+from jax.experimental import pallas as pl
+from jax.experimental.pallas import tpu as pltpu
 from jax.sharding import PartitionSpec as P
 
 EPSILON = 1e-06
 
 
-def pl_ceil(total, step):
-    return -(-total // step)
+def weight_body(d_ref, packed_ref, chan_ref, out_ref):
+    acc = lax.dot_general(
+        d_ref[...], packed_ref[...], (((0,), (0,)), ((), ())), preferred_element_type=jnp.float32
+    )
+    edge = acc.shape[1] - chan_ref.shape[1]
+    out_ref[...] = acc
+    out_ref[:, edge:] = acc[:, edge:] + chan_ref[...]
+
+
+def weight_grad(d_stem_low, packed_wide, chan_edge):
+    tokens, channels = d_stem_low.shape
+    width = packed_wide.shape[1]
+    block = 896
+    return pl.pallas_call(
+        weight_body,
+        grid=(channels // block,),
+        in_specs=[
+            pl.BlockSpec((tokens, block), lambda i: (0, i)),
+            pl.BlockSpec((tokens, width), lambda i: (0, 0)),
+            pl.BlockSpec((block, chan_edge.shape[1]), lambda i: (i, 0)),
+        ],
+        out_specs=pl.BlockSpec((block, width), lambda i: (i, 0)),
+        out_shape=jax.ShapeDtypeStruct((channels, width), jnp.float32),
+    )(d_stem_low, packed_wide, chan_edge)
+
+
+def back_body(
+    mask_ref, mask_wide_ref, slope_ref, normed_ref, stem_ref, inv_ref, gain_ref, kern_ref,
+    gated_ref, row_ref, chan_ref,
+):
+    rows = 32
+    slot_total = stem_ref.shape[0] // rows
+    cols = stem_ref.shape[1]
+
+    @pl.when(pl.program_id(0) == 0)
+    def _():
+        row_ref[...] = jnp.zeros_like(row_ref)
+
+    gain = gain_ref[...]
+    taps = [kern_ref[k : k + 1, :] for k in range(5)]
+    gain_acc = jnp.zeros((8, cols), jnp.float32)
+    kern_acc = [jnp.zeros((8, cols), jnp.float32) for _ in range(5)]
+
+    def fold(v):
+        return v[0:8] + v[8:16] + v[16:24] + v[24:32]
+
+    for g in range(slot_total):
+        here = slice(g * rows, (g + 1) * rows)
+        d = jnp.zeros((rows, cols), jnp.float32)
+        for k in range(5):
+            p = g + 4 - k
+            d = d + slope_ref[p * rows : (p + 1) * rows, :].astype(jnp.float32) * (
+                mask_wide_ref[p, k] * taps[k]
+            )
+        unit = stem_ref[here, :] * inv_ref[here, :]
+        gated = d * gain
+        gated_ref[here, :] = gated
+        row_ref[here, :] += jnp.sum(gated * unit, axis=1, keepdims=True)
+        gain_acc = gain_acc + fold(d * unit)
+        own = slope_ref[(g + 2) * rows : (g + 3) * rows, :].astype(jnp.float32)
+        for k in range(5):
+            q = g + k
+            prod = own * normed_ref[q * rows : (q + 1) * rows, :].astype(jnp.float32)
+            kern_acc[k] = kern_acc[k] + mask_ref[g, k] * fold(prod)
+    chan_ref[0:1, :] = jnp.sum(gain_acc, axis=0, keepdims=True)
+    for k in range(5):
+        chan_ref[k + 1 : k + 2, :] = jnp.sum(kern_acc[k], axis=0, keepdims=True)
+    chan_ref[6:8, :] = jnp.zeros((2, cols), jnp.float32)
+
+
+def back_pass(clip_mask, mask_padded, slope_padded, padded, stem_out, inv_rms, gain, kernel):
+    tokens, channels = stem_out.shape
+    wide = slope_padded.shape[0]
+    block = 512
+    whole = pl.BlockSpec(memory_space=pltpu.SMEM)
+
+    def columns(rows):
+        return pl.BlockSpec((rows, block), lambda i: (0, i))
+
+    row_spec = pl.BlockSpec((tokens, 1), lambda i: (0, 0))
+    return pl.pallas_call(
+        back_body,
+        grid=(channels // block,),
+        in_specs=[
+            whole, whole, columns(wide), columns(wide), columns(tokens), row_spec, columns(1),
+            columns(5),
+        ],
+        out_specs=[columns(tokens), row_spec, columns(8)],
+        out_shape=[
+            jax.ShapeDtypeStruct((tokens, channels), jnp.float32),
+            jax.ShapeDtypeStruct((tokens, 1), jnp.float32),
+            jax.ShapeDtypeStruct((8, channels), jnp.float32),
+        ],
+    )(clip_mask, mask_padded, slope_padded, padded, stem_out, inv_rms, gain, kernel)
 
 
 def extended_2(cells, sides, width):
@@ -52,34 +146,6 @@
         )
         result = result + addend
     return result
-
-
-def temporal_back(slope_padded, mask_padded, kernel, slot_total):
-    kernel_wide = kernel.astype(jnp.float32)
-    result = jnp.zeros((slot_total,) + slope_padded.shape[1:], jnp.float32)
-    for offset in range(5):
-        first_row = 4 - offset
-        weights_row = (
-            mask_padded[first_row : first_row + slot_total, offset][:, None, None]
-            * kernel_wide[offset][None, None, :]
-        )
-        result = (
-            result
-            + slope_padded[first_row : first_row + slot_total].astype(jnp.float32) * weights_row
-        )
-    return result
-
-
-def kernel_sums(slope_blocks, padded, clip_mask, slot_total):
-    stacked = []
-    for offset in range(5):
-        product = jnp.sum(
-            slope_blocks.astype(jnp.float32)
-            * padded[offset : offset + slot_total].astype(jnp.float32),
-            axis=1,
-        )
-        stacked.append(jnp.sum(product * clip_mask[:, offset][:, None], axis=0))
-    return jnp.stack(stacked, axis=0)
 
 
 def rim_rows(values, margin):
@@ -145,7 +211,8 @@
     extended = seq_index * slot_count + jnp.arange(-2, slot_count + 2, dtype=jnp.int32)
     clip_mask = slot_mask(segment_row, centre)
     mask_padded = slot_mask(segment_row, extended)
-    padded = rim_rows(normed, 2 * slot_rows).reshape(slot_count + 4, slot_rows, channels)
+    padded_rows = rim_rows(normed, 2 * slot_rows)
+    padded = padded_rows.reshape(slot_count + 4, slot_rows, channels)
     mixed_rows = temporal_mix(padded, clip_mask, kernel_full, slot_count).reshape(tokens, channels)
     features = (stem_out + jax.nn.silu(mixed_rows)).astype(jnp.bfloat16)
     upstream_wide = cotangent[0].astype(jnp.float32)
@@ -153,40 +220,41 @@
     slope_low = (upstream_wide * gate_value * (1.0 + mixed_rows * (1.0 - gate_value))).astype(
         jnp.bfloat16
     )
-    slope_padded = rim_rows(slope_low, 2 * slot_rows).reshape(slot_count + 4, slot_rows, channels)
-    d_normed = temporal_back(slope_padded, mask_padded, kernel_full, slot_count).reshape(
-        tokens, channels
-    )
-    gated = d_normed * gain_wide
+    slope_rows = rim_rows(slope_low, 2 * slot_rows)
+    gated, row_sum, chan_rows = back_pass(
+        clip_mask,
+        mask_padded,
+        slope_rows,
+        padded_rows,
+        stem_out,
+        inv_rms,
+        gain_wide[None, :],
+        kernel_full.astype(jnp.float32),
+    )
     d_stem = upstream_wide + inv_rms * (
-        gated - unit_rows * jnp.mean(gated * unit_rows, axis=1, keepdims=True)
+        gated - unit_rows * (row_sum / channels)
     )
     d_stem_low = d_stem.astype(jnp.bfloat16)
     grad_rows = jnp.dot(d_stem_low, weight_full, preferred_element_type=jnp.float32).astype(
         jnp.bfloat16
     )
-    gain_part = jnp.sum(d_normed * unit_rows, axis=0)
-    slope_blocks = slope_padded[2 : 2 + slot_count]
-    kernel_part = kernel_sums(slope_blocks, padded, clip_mask, slot_count)
-    chan_terms = jnp.concatenate([gain_part[None, :], kernel_part], axis=0).T
-    weight_block = lax.dot_general(
-        d_stem_low,
-        jnp.pad(packed, ((0, 0), (0, 6))),
-        (((0,), (0,)), ((), ())),
-        preferred_element_type=jnp.float32,
-    )
-    total_block = weight_block + jnp.pad(chan_terms, ((0, 0), (pixel_width, 0)))
+    chan_edge = jnp.pad(chan_rows[:6].T, ((0, 0), (24, 0)))
+    total_block = weight_grad(d_stem_low, jnp.pad(packed, ((0, 0), (0, 6))), chan_edge)
+    shard = lax.psum_scatter(total_block, "fsdp", scatter_dimension=0, tiled=True)
     panel = channels // fsdp_size
-    panel_padded = 16 * seq_size * pl_ceil(panel, 16 * seq_size)
-    stacked = jnp.pad(
-        total_block.reshape(fsdp_size, panel, pixel_width + 6),
-        ((0, 0), (0, panel_padded - panel), (0, 0)),
-    ).reshape(fsdp_size * panel_padded, pixel_width + 6)
-    piece = lax.psum_scatter(stacked, ("fsdp", "seq"), scatter_dimension=0, tiled=True)
+    part_rows = 16
+    width = pixel_width + 6
+    parts = jnp.pad(shard.astype(jnp.bfloat16), ((0, part_rows * seq_size - panel), (0, 0)))
+    spread = lax.all_to_all(parts, "seq", split_axis=0, concat_axis=0, tiled=True)
     grad_scale = 1.0 / math.sqrt(tokens * seq_size * fsdp_size)
-    summed = lax.all_gather(piece * grad_scale, "seq", axis=0, tiled=True)[:panel]
-    grad_weight = summed[:, :pixel_width].astype(jnp.bfloat16)
-    grad_channels = summed[:, pixel_width:].T
+    piece = jnp.sum(spread.reshape(seq_size, part_rows, width).astype(jnp.float32), axis=0)
+    piece = (piece * grad_scale).astype(jnp.bfloat16)
+    copies = jnp.broadcast_to(piece[None], (seq_size, part_rows, width))
+    summed = lax.all_to_all(
+        copies.reshape(seq_size * part_rows, width), "seq", split_axis=0, concat_axis=0, tiled=True
+    )[:panel]
+    grad_weight = summed[:, :pixel_width]
+    grad_channels = summed[:, pixel_width:].astype(jnp.float32).T
     return (features[None], grad_rows[None], grad_weight, grad_channels)
 
 

time: 1610 us -> 339 us (0.21)
  waiting for transfers between devices: 1380 us -> 154 us
  other arithmetic: 89.6 us -> 35 us
  local copies, waits for them, and re-layouts: 71.6 us -> 36.1 us
  Pallas kernels: 0 us -> 33.2 us
  blocking collectives: 0 us -> 20.9 us
    reduce_scatter x1, waiting for transfers between devices: 1230 us -> 108 us  [shards(): lax.psum_scatter(total_block, 'fsdp', scatter_dimension=0, tiled=True)]
    all_gather x1 -> x0, waiting for transfers between devices: 108 us -> none  [shards(): lax.all_gather(piece * grad_scale, 'seq', axis=0, tiled=True)[:panel]]
    mul x9 -> x3, other arithmetic: 40.1 us -> 0.32 us  [the longest x2 0.23 us: temporal_mix(): clip_mask[:, offset][:, None, None] * kernel_wide[offset][None, None, :]]
    pallas_call x0 -> x2, Pallas kernels: none -> 33.2 us  [the longest x1 20.7 us: back_pass(): pl.pallas_call(back_body, grid=(channels // block,), in_specs=[whole, who...]
    reduce_sum x11 -> x1, other arithmetic: 24.4 us -> 0.1 us  [shards(): jnp.sum(spread.reshape(seq_size, part_rows, width).astype(jnp.float32), a...]
    all_to_all x0 -> x1, blocking collectives: none -> 20.9 us  [shards(): lax.all_to_all(parts, 'seq', split_axis=0, concat_axis=0, tiled=True)]
    add x1 -> x0, local copies, waits for them, and re-layouts: 18.8 us -> none  [shards(): total_block = weight_block + jnp.pad(chan_terms, ((0, 0), (pixel_width, 0)))]
  transfers between devices with their start and end apart: 9 -> 9, of which waited for: 5 -> 7; matrix products, arithmetic and copies ran while one was open for 4% -> 12% of each run, Pallas kernels for 0% -> 0%
where the time goes in v2:
time: 339 us; the launch traced here: 338 us
  waiting for transfers between devices  154 us (45%)
  local copies, waits for them, and re-layouts  36.1 us (11%)
  other arithmetic  35 us (10%)
  Pallas kernels  33.2 us (10%)
  starting transfers between devices  25.7 us (8%)
  blocking collectives  20.9 us (6%)
  matrix products  18.4 us (5%)
  between operations  14.5 us (4%)
    reduce_scatter x1, waiting for transfers between devices, shards(): lax.psum_scatter(total_block, 'fsdp', scatter_dimension=0, tiled=True)  108 us
    all_to_all x1, waiting for transfers between devices, shards(): lax.all_to_all(outbox, 'seq', split_axis=0, concat_axis=0, tiled=True)  27.7 us
    all_to_all x1, blocking collectives, shards(): lax.all_to_all(parts, 'seq', split_axis=0, concat_axis=0, tiled=True)  20.9 us
    pallas_call x1, Pallas kernels, back_pass(): pl.pallas_call(back_body, grid=(channels // block,), in_specs=[whole, who...  20.7 us
    convert_element_type x1, other arithmetic, shards(): d_stem_low = d_stem.astype(jnp.bfloat16)  14.4 us
    pallas_call x1, Pallas kernels, weight_grad(): pl.pallas_call(weight_body, grid=(channels // block,), in_specs=[pl.Block...  12.5 us
    dot_general x1, matrix products, shards(): jnp.dot(d_stem_low, weight_full, preferred_element_type=jnp.float32)  10.4 us
    ppermute x2, waiting for transfers between devices, extended_2(): lax.ppermute(head, axis, [((i + 1) % count, i) for i in range(ends)])  8.56 us
  transfers between devices with their start and end apart: 9, of which 7 were waited for; matrix products, arithmetic and copies ran while one was open for 12% of the time, Pallas kernels for 0%

profile of v2, /device:TPU:32, one launch (start us, length us, event | category | flops | bytes accessed | tf_op | source)
XLA Modules:
  0.0 338.2 jit_solution(11748885764900597838)
XLA Ops:
  7.2 0.7 broadcast_in_dim.26
  8.0 0.8 copy.69
  8.8 1.9 concatenate.17
  12.1 0.9 convert_reduce_fusion.1
  15.0 7.0 %all-to-all-start = ((bf16[16,2,1]{1,2,0:T(2,128)(2,1)}), bf16[16,2,1]{1,2,0:T(2,128)(2,1)S(1)}, u32[]{:S(2)}, u32[]{:S(2)}) async-start(bf16[16,2,1]{1,2,0:T(2,128)(2,1)} %all_to_all.28), calls=%async_computation | async-start | bytes 16384 | tf_op jit(solution)/shard_map/all_to_all | solution.py:184
  22.2 1.8 broadcast_in_dim.21
  24.0 6.5 %scatter_fusion = bf16[32,32,1176]{2,1,0:T(8,128)(2,1)} fusion(bf16[32,32,1176]{2,1,0:T(8,128)(2,1)} %broadcast_in_dim.21, s32[17]{0:T(128)S(1)} %fusion.28, bf16[17,32,1176]{2,1,0:T(8,128)(2,1)} %bitcast.121), kind=kCustom, calls=%fused_computation.11 | custom fusion | bytes 3838532 | tf_op jit(solution)/shard_map/scatter | solution.py:174
  30.5 7.2 %all-to-all-start.1 = ((bf16[32,32,1176]{2,1,0:T(8,128)(2,1)}), bf16[32,32,1176]{2,1,0:T(8,128)(2,1)}, u32[]{:S(2)}, u32[]{:S(2)}) async-start(bf16[32,32,1176]{2,1,0:T(8,128)(2,1)} %scatter_fusion), calls=%async_computation.1 | async-start | bytes 5242880 | tf_op jit(solution)/shard_map/all_to_all | solution.py:183
  37.7 0.7 gather_fusion
  38.4 0.7 gather_fusion.5
  39.1 0.7 gather_fusion.9
  39.8 0.7 gather_fusion.8
  40.6 0.7 gather_fusion.7
  41.3 0.7 gather_fusion.1
  42.8 0.7 gather_fusion.3
  43.5 0.7 gather_fusion.4
  46.6 27.7 %all-to-all-done.1 = bf16[32,32,1176]{2,1,0:T(8,128)(2,1)} async-done(((bf16[32,32,1176]{2,1,0:T(8,128)(2,1)}), bf16[32,32,1176]{2,1,0:T(8,128)(2,1)}, u32[]{:S(2)}, u32[]{:S(2)}) %all-to-all-start.1) | async-done | bytes 2408480 | tf_op jit(solution)/shard_map/all_to_all | solution.py:183
  74.4 4.2 %scatter_fusion.1 = bf16[18,32,1176]{2,1,0:T(8,128)(2,1)S(1)} fusion(bf16[18,32,1176]{2,1,0:T(8,128)(2,1)S(1)} %broadcast_in_dim.18, s32[32]{0:T(128)S(1)} %fusion.30, bf16[32,32,1176]{2,1,0:T(8,128)(2,1)} %all-to-all-done.1), kind=kCustom, calls=%fused_computation.12 | custom fusion | bytes 7225472 | tf_op jit(solution)/shard_map/scatter | solution.py:191
  78.8 1.2 pad.12.packed_ref
  80.0 1.5 slice.119
  82.1 8.0 %multiply_reduce_fusion = (f32[544]{0:T(1024)S(1)}, f32[544,3584]{1,0:T(8,128)S(1)}) fusion(bf16[544,1176]{1,0:T(8,128)(2,1)S(1)} %bitcast.117, bf16[3584,1182]{1,0:T(8,128)(2,1)} %all-gather.2.cloned.1.call-done), kind=kOutput, calls=%fused_computation.34 | convolution fusion | flops 4589583872 | bytes 17553024 | tf_op jit(solution)/shard_map/dot_general | solution.py:203
  90.2 0.8 rsqrt.7.inv_ref
  91.0 1.3 multiply_convert_fusion
  92.4 2.8 collective-permute-start
  95.2 1.3 collective-permute-start.1
  97.4 5.0 %collective-permute-done = bf16[64,3584]{1,0:T(8,128)(2,1)S(1)} collective-permute-done((bf16[64,3584]{1,0:T(8,128)(2,1)S(1)}, bf16[64,3584]{1,0:T(8,128)(2,1)S(1)}, u32[]{:S(2)}, u32[]{:S(2)}) %collective-permute-start) | collective-permute-done | bytes 458784 | tf_op jit(solution)/shard_map/ppermute | solution.py:117
  102.4 4.1 %collective-permute-done.1 = bf16[64,3584]{1,0:T(8,128)(2,1)S(1)} collective-permute-done((bf16[64,3584]{1,0:T(8,128)(2,1)S(1)}, bf16[64,3584]{1,0:T(8,128)(2,1)S(1)}, u32[]{:S(2)}, u32[]{:S(2)}) %collective-permute-start.1) | collective-permute-done | bytes 458784 | tf_op jit(solution)/shard_map/ppermute | solution.py:119
  106.5 7.6 %fusion.5 = (bf16[544,3584]{1,0:T(8,128)(2,1)S(1)}, f32[544,3584]{1,0:T(8,128)}) fusion(bf16[1,544,3584]{2,1,0:T(8,128)(2,1)S(1)} %copy-done.3, f32[17,3584]{1,0:T(8,128)S(1)} %get-tuple-element.67, bf16[64,3584]{1,0:T(8,128)(2,1)S(1)} %collective-permute-done.1, bf16[544,3584]{1,0:T(8,128)(2,1)S(1)} %multiply_convert_fusion, ...), kind=kLoop, calls=%fused_computation.20 | loop fusion | flops 70189056 | bytes 21633024 | tf_op jit(solution)/shard_map/convert_element_type | solution.py:220
  114.2 2.2 collective-permute-start.2
  116.4 1.5 collective-permute-start.3
  117.9 2.4 pad_maximum_fusion.1.normed_ref
  120.3 2.1 collective-permute-done.2
  122.4 4.4 %collective-permute-done.3 = bf16[64,3584]{1,0:T(8,128)(2,1)S(1)} collective-permute-done((bf16[64,3584]{1,0:T(8,128)(2,1)S(1)}, bf16[64,3584]{1,0:T(8,128)(2,1)S(1)}, u32[]{:S(2)}, u32[]{:S(2)}) %collective-permute-start.3) | collective-permute-done | bytes 458784 | tf_op jit(solution)/shard_map/ppermute | solution.py:119
  126.8 2.4 pad_maximum_fusion.slope_ref
  129.2 20.7 %shard_map.102 = (f32[544,3584]{1,0:T(8,128)}, f32[544,1]{1,0:T(8,128)}, f32[8,3584]{1,0:T(8,128)}) custom-call(f32[17,5]{1,0:T(8,128)} %copy.72.mask_ref, f32[21,5]{1,0:T(8,128)} %copy.73.mask_wide_ref, bf16[672,3584]{1,0:T(8,128)(2,1)} %pad_maximum_fusion.slope_ref, bf16[672,3584]{1,0:T(8,128)(2,1)} %pad_maximum_fusion.1.normed_ref, ...), custom_call_target="tpu_custom_call" | custom-call | tf_op jit(solution)/shard_map/pallas_call | solution.py:93
  149.9 1.1 multiply_reduce_fusion.1
  151.0 1.5 copy.75
  152.5 1.8 pad.13.chan_ref
  154.3 14.4 %fusion.6 = (bf16[544,3584]{1,0:T(8,128)(2,1)}, bf16[1,544,3584]{2,1,0:T(8,128)(2,1)}) fusion(f32[544,3584]{1,0:T(8,128)} %get-tuple-element.7, f32[544,3584]{1,0:T(8,128)} %copy-done.2, bf16[1,544,3584]{2,1,0:T(8,128)(2,1)} %param.13, f32[544]{0:T(1024)S(1)} %multiply_reduce_fusion.1, f32[544]{0:T(1024)S(1)} %add_rsqrt_fusion, f32[544,3584]{1,0:T(8,128)} %get-tuple-element.40), kind=kLoop, calls=%fused_computation.21 | loop fusion | flops 25346048 | bytes 35098880 | tf_op jit(solution)/shard_map/convert_element_type | solution.py:237
  168.7 12.5 %shard_map.103 = f32[3584,1182]{1,0:T(8,128)} custom-call(bf16[544,3584]{1,0:T(8,128)(2,1)} %get-tuple-element.43.d_ref, bf16[544,1182]{1,0:T(8,128)(2,1)} %pad.12.packed_ref, f32[3584,30]{1,0:T(8,128)} %pad.13.chan_ref), custom_call_target="tpu_custom_call" | custom-call | tf_op jit(solution)/shard_map/pallas_call | solution.py:26
  181.2 108.2 %reduce-scatter.2.cloned.1.call-done = f32[224,1182]{1,0:T(8,128)} async-done(((f32[3584,1182]{1,0:T(8,128)}), f32[224,1182]{1,0:T(8,128)}) %reduce-scatter.2.cloned.1.call-update) | async-done | bytes 1059088 | tf_op jit(solution)/shard_map/reduce_scatter | solution.py:243
  289.5 1.3 convert_element_type.236
  290.8 20.9 %all_to_all.33 = bf16[16,16,1182]{2,1,0:T(8,128)(2,1)S(1)} all-to-all(bf16[16,16,1182]{2,1,0:T(8,128)(2,1)S(1)} %bitcast.118), channel_id=1, replica_groups=mesh['seq'=16,'fsdp'=16] {'seq'}, dimensions={0} | all-to-all | bytes 1210368 | tf_op jit(solution)/shard_map/all_to_all | solution.py:248
  311.9 0.9 broadcast_in_dim.25
  312.8 3.7 %all-to-all-start.3 = ((bf16[16,16,1182]{2,1,0:T(8,128)(2,1)}), bf16[16,16,1182]{2,1,0:T(8,128)(2,1)S(1)}, u32[]{:S(2)}, u32[]{:S(2)}) async-start(bf16[16,16,1182]{2,1,0:T(8,128)(2,1)} %broadcast_in_dim.25), calls=%async_computation.4 | async-start | bytes 1310720 | tf_op jit(solution)/shard_map/all_to_all | solution.py:253
  316.5 10.4 %fusion.17 = bf16[1,544,1176]{2,1,0:T(8,128)(2,1)} fusion(bf16[544,3584]{1,0:T(8,128)(2,1)} %get-tuple-element.43.d_ref, bf16[3584,1182]{1,0:T(8,128)(2,1)} %all-gather.2.cloned.1.call-done), kind=kOutput, calls=%fused_computation.47 | convolution fusion | flops 4586324992 | bytes 13651456 | tf_op jit(solution)/shard_map/dot_general | solution.py:238
  327.0 2.8 all-to-all-done.3
  329.8 0.8 slice.135
  (76 shorter events, 9.5 us)
Async XLA Ops:
  7.2 30.5 %copy-start = (s32[1,272]{1,0:T(1,128)S(1)}, s32[1,272]{1,0:T(1,128)}, u32[]{:S(2)}) copy-start(s32[1,272]{1,0:T(1,128)} %param.9) | copy-start | bytes 3268
  7.2 72.8 %all-gather.2.cloned.1.call-start = ((), (), s32[]{:S(2)}) async-start(), calls=%async_computation.5 | async-start | bytes 9748480 | tf_op jit(solution)/shard_map/all_gather | solution.py:196
  15.0 15.4 %all-to-all-start = ((bf16[16,2,1]{1,2,0:T(2,128)(2,1)}), bf16[16,2,1]{1,2,0:T(2,128)(2,1)S(1)}, u32[]{:S(2)}, u32[]{:S(2)}) async-start(bf16[16,2,1]{1,2,0:T(2,128)(2,1)} %all_to_all.28), calls=%async_computation | async-start | bytes 16384 | tf_op jit(solution)/shard_map/all_to_all | solution.py:184
  30.5 43.8 %all-to-all-start.1 = ((bf16[32,32,1176]{2,1,0:T(8,128)(2,1)}), bf16[32,32,1176]{2,1,0:T(8,128)(2,1)}, u32[]{:S(2)}, u32[]{:S(2)}) async-start(bf16[32,32,1176]{2,1,0:T(8,128)(2,1)} %scatter_fusion), calls=%async_computation.1 | async-start | bytes 5242880 | tf_op jit(solution)/shard_map/all_to_all | solution.py:183
  37.6 251.9 %reduce-scatter.2.cloned.1.call-start = ((), (), s32[]{:S(2)}) async-start(), calls=%async_computation.6 | async-start | bytes 19496960 | tf_op jit(solution)/shard_map/reduce_scatter | solution.py:243
  81.9 8.2 %copy-start.4 = (f32[5,3584]{1,0:T(8,128)}, f32[5,3584]{1,0:T(8,128)S(1)}, u32[]{:S(2)}) copy-start(f32[5,3584]{1,0:T(8,128)S(1)} %slice_convert_fusion.kern_ref) | copy-start | bytes 215044
  90.1 6.7 %copy-start.2 = (f32[544,3584]{1,0:T(8,128)}, f32[544,3584]{1,0:T(8,128)S(1)}, u32[]{:S(2)}) copy-start(f32[544,3584]{1,0:T(8,128)S(1)} %get-tuple-element.64.stem_ref) | copy-start | bytes 23396356
  90.2 16.4 %copy-start.3 = (bf16[1,544,3584]{2,1,0:T(8,128)(2,1)S(1)}, bf16[1,544,3584]{2,1,0:T(8,128)(2,1)}, u32[]{:S(2)}) copy-start(bf16[1,544,3584]{2,1,0:T(8,128)(2,1)} %param.13) | copy-start | bytes 11698180
  92.4 10.0 %collective-permute-start = (bf16[64,3584]{1,0:T(8,128)(2,1)S(1)}, bf16[64,3584]{1,0:T(8,128)(2,1)S(1)}, u32[]{:S(2)}, u32[]{:S(2)}) collective-permute-start(bf16[64,3584]{1,0:T(8,128)(2,1)S(1)} %get-tuple-element.47), channel_id=1, source_target_pairs={{0,16},{16,32},{32,48},{48,64},{64,80},{80,96},{96,112},{112,128},... | collective-permute-start | bytes 1376264 | tf_op jit(solution)/shard_map/ppermute | solution.py:117
  95.2 11.4 %collective-permute-start.1 = (bf16[64,3584]{1,0:T(8,128)(2,1)S(1)}, bf16[64,3584]{1,0:T(8,128)(2,1)S(1)}, u32[]{:S(2)}, u32[]{:S(2)}) collective-permute-start(bf16[64,3584]{1,0:T(8,128)(2,1)S(1)} %get-tuple-element.48), channel_id=1, source_target_pairs={{16,0},{32,16},{48,32},{64,48},{80,64},{96,80},{112,96},{128,112},... | collective-permute-start | bytes 1376264 | tf_op jit(solution)/shard_map/ppermute | solution.py:119
  114.2 8.2 %collective-permute-start.2 = (bf16[64,3584]{1,0:T(8,128)(2,1)S(1)}, bf16[64,3584]{1,0:T(8,128)(2,1)S(1)}, u32[]{:S(2)}, u32[]{:S(2)}) collective-permute-start(bf16[64,3584]{1,0:T(8,128)(2,1)S(1)} %get-tuple-element.45), channel_id=1, source_target_pairs={{0,16},{16,32},{32,48},{48,64},{64,80},{80,96},{96,112},{112,128},... | collective-permute-start | bytes 1376264 | tf_op jit(solution)/shard_map/ppermute | solution.py:117
  116.4 10.4 %collective-permute-start.3 = (bf16[64,3584]{1,0:T(8,128)(2,1)S(1)}, bf16[64,3584]{1,0:T(8,128)(2,1)S(1)}, u32[]{:S(2)}, u32[]{:S(2)}) collective-permute-start(bf16[64,3584]{1,0:T(8,128)(2,1)S(1)} %get-tuple-element.46), channel_id=1, source_target_pairs={{16,0},{32,16},{48,32},{64,48},{80,64},{96,80},{112,96},{128,112},... | collective-permute-start | bytes 1376264 | tf_op jit(solution)/shard_map/ppermute | solution.py:119
  312.8 17.0 %all-to-all-start.3 = ((bf16[16,16,1182]{2,1,0:T(8,128)(2,1)}), bf16[16,16,1182]{2,1,0:T(8,128)(2,1)S(1)}, u32[]{:S(2)}, u32[]{:S(2)}) async-start(bf16[16,16,1182]{2,1,0:T(8,128)(2,1)} %broadcast_in_dim.25), calls=%async_computation.4 | async-start | bytes 1310720 | tf_op jit(solution)/shard_map/all_to_all | solution.py:253
  316.5 14.8 %copy-start.1 = (s32[1,272]{1,0:T(1,128)S(1)}, s32[1,272]{1,0:T(1,128)}, u32[]{:S(2)}) copy-start(s32[1,272]{1,0:T(1,128)} %param.9) | copy-start | bytes 3268
Sparse Core Ops, SparseCore 0:
  10.9 60.3 all-gather.1
  181.3 108.0 reduce-scatter.1
